TPU v7x, 32 devices: a whole 2x2x4 slice. The times are simulated.
32 devices in a mesh: blk: 8 (over z, y), rep: 4 (over x, core).
Axes of the slice: x: 2, y: 2, z: 4, core: 2. Of those that a mesh axis runs over, the one named last changes fastest.
Arguments:
- features: bfloat16 [8192, 256], P(('blk', 'rep')), may hold values from -6 to 6
- tiles: bfloat16 [8, 64, 128, 128], P('blk', 'rep'), may hold values from -0.25 to 0.25
- tile_rows: int32 [8, 64], P('blk', 'rep'), may hold values from 0 to 7
- tile_cols: int32 [8, 64], P('blk', 'rep'), may hold values from 0 to 15
- counts: int32 [8, 4], P('blk', 'rep'), may hold values from 4 to 16
- weight: bfloat16 [256, 256], replicated, may hold values from -0.375 to 0.375
- bias: float32 [256], replicated, may hold values from -3 to 3
- cotangent: bfloat16 [8192, 256], P(('blk', 'rep')), may hold values from -6 to 6
Outputs:
- activations: bfloat16 [8192, 256], P(('blk', 'rep'))
- feature_grad: bfloat16 [8192, 256], P(('blk', 'rep'))
- weight_grad: float32 [256, 256], replicated
- bias_grad: float32 [256], replicated
All inputs are finite; a program needn't handle non-finite values.
Results may differ from a plain program's by a relative error of at most 0.006.
Values may be sent and summed in bfloat16 or wider, within the bound.
A program may use at most 64 MiB of HBM per device.

v0:
```python
import jax
import jax.numpy as jnp
from jax import lax
from jax.sharding import PartitionSpec as P


def shifted(block, axis, distance):
    devices = range(lax.axis_size(axis))
    route = [((i - distance) % len(devices), i) for i in devices]
    return lax.ppermute(block, axis, route)


def per_device(features, tiles, tile_rows, tile_cols, counts, weight, bias, cotangent):
    highest = lax.Precision.HIGHEST
    tile_size = tiles.shape[2]
    slot_count = tiles.shape[1]
    feat_width = features.shape[1]
    own_rows = features.shape[0]
    own_tiles = own_rows // tile_size
    rep_count = lax.axis_size("rep")
    blk_count = lax.axis_size("blk")
    slot_tiles = tiles[0]
    row_index = tile_rows[0]
    col_index = tile_cols[0]
    slot_live = (jnp.arange(slot_count, dtype=jnp.int32) < counts[0, 0]).astype(jnp.float32)
    wanted = col_index[:, None] * tile_size + jnp.arange(tile_size, dtype=jnp.int32)[None, :]
    piece = lax.all_gather(features, "blk", axis=0, tiled=True)
    piece_count = piece.shape[0]
    inside = (wanted >= 0) & (wanted < piece_count)
    clipped = jnp.clip(wanted, 0, piece_count - 1)
    taken = jnp.take(piece, clipped.reshape(-1), axis=0).reshape(slot_count, tile_size, feat_width)
    selected = jnp.where(inside[:, :, None], taken, jnp.zeros((), jnp.bfloat16))
    partial_value = jnp.einsum(
        "sij,sjf->sif", slot_tiles, selected, preferred_element_type=jnp.float32
    )
    row_onehot = (
        row_index[:, None] == jnp.arange(rep_count * own_tiles, dtype=jnp.int32)[None, :]
    ).astype(jnp.float32) * slot_live[:, None]
    summed = jnp.einsum("st,sif->tif", row_onehot, partial_value, precision=highest)
    aggregate = lax.psum_scatter(
        summed.reshape(rep_count * own_rows, feat_width), "rep", scatter_dimension=0, tiled=True
    ).astype(jnp.bfloat16)
    pre_act = jnp.dot(aggregate, weight, preferred_element_type=jnp.float32) + bias[None, :]
    logistic = jax.nn.sigmoid(pre_act)
    activations = (pre_act * logistic).astype(jnp.bfloat16)
    act_grad = (
        cotangent.astype(jnp.float32) * logistic * (1.0 + pre_act * (1.0 - logistic))
    ).astype(jnp.bfloat16)
    local_weight = jnp.dot(aggregate.T, act_grad, preferred_element_type=jnp.float32)
    local_bias = jnp.sum(act_grad.astype(jnp.float32), axis=0)
    weight_grad, bias_grad = lax.psum((local_weight, local_bias), ("blk", "rep"))
    scale_factor = 1.0 / (blk_count * rep_count)
    weight_grad = weight_grad * scale_factor
    bias_grad = bias_grad * scale_factor
    agg_grad = jnp.dot(act_grad, weight.T, preferred_element_type=jnp.float32).astype(jnp.bfloat16)
    gathered = lax.all_gather(agg_grad, "rep", axis=0, tiled=True).reshape(
        rep_count * own_tiles, tile_size, feat_width
    )
    chosen = jnp.take(gathered, row_index, axis=0)
    contribution = (
        jnp.einsum("sij,sif->sjf", slot_tiles, chosen, preferred_element_type=jnp.float32)
        * slot_live[:, None, None]
    )

    def column_terms(first_row, row_count):
        targets = first_row // tile_size + jnp.arange(row_count // tile_size, dtype=jnp.int32)
        col_onehot = (col_index[:, None] == targets[None, :]).astype(jnp.float32)
        placed = jnp.einsum("sp,sjf->pjf", col_onehot, contribution, precision=highest)
        return placed.reshape(row_count, feat_width)

    own_block = lax.axis_index("blk")

    def travel_step(step_index, travelling):
        source_block = (own_block - step_index) % blk_count
        travelling = travelling + column_terms(source_block * own_rows, own_rows)
        return shifted(travelling, "blk", 1)

    feature_sum = lax.fori_loop(
        0, blk_count, travel_step, jnp.zeros((own_rows, feat_width), jnp.float32)
    )
    feature_grad = feature_sum.astype(jnp.bfloat16)
    return (activations, feature_grad, weight_grad, bias_grad)


def solution(mesh):
    in_specs = (
        P(("blk", "rep"), None),
        P("blk", "rep", None, None),
        P("blk", "rep"),
        P("blk", "rep"),
        P("blk", "rep"),
        P(),
        P(),
        P(("blk", "rep"), None),
    )
    out_specs = (P(("blk", "rep"), None), P(("blk", "rep"), None), P(), P())
    return jax.shard_map(
        per_device, mesh=mesh, in_specs=in_specs, out_specs=out_specs, check_vma=False
    )
```

profile of v0, /device:TPU:10, one launch (start us, length us, event | category | flops | bytes accessed | tf_op | source)
XLA Modules:
  0.0 242.8 jit_solution(17766153802447288838)
XLA Ops:
  9.5 40.9 %all-gather.2.cloned.1.call-done = bf16[2048,256]{1,0:T(8,128)(2,1)} async-done(((bf16[256,256]{1,0:T(8,128)(2,1)}), bf16[2048,256]{1,0:T(8,128)(2,1)}) %all-gather.2.cloned.1.call-update) | async-done | bytes 1048592 | tf_op jit(solution)/shard_map/all_gather | solution.py:27
  50.4 9.8 %gather_fusion = bf16[2048,256]{1,0:T(8,128)(2,1)} fusion(bf16[2048,256]{1,0:T(8,128)(2,1)} %all-gather.2.cloned.1.call-done, s32[2048]{0:T(1024)S(1)} %broadcast_clamp_fusion), kind=kCustom, calls=%fused_computation | custom fusion | bytes 2105344 | tf_op jit(solution)/shard_map/jit(_take)/gather | solution.py:31
  60.2 2.3 fusion.8
  62.6 2.1 copy.18
  64.7 2.7 %fusion.5 = f32[8,128,256]{2,0,1:T(8,128)S(1)} fusion(f32[16,256,128]{1,0,2:T(8,128)} %copy.18, f32[16]{0:T(128)S(1)} %compare_convert_fusion, s32[16]{0:T(128)S(1)} %bitcast.53), kind=kOutput, calls=%fused_computation.9 | convolution fusion | flops 50331904 | bytes 3145856 | tf_op jit(solution)/shard_map/st,sif->tif/dot_general | solution.py:39
  67.4 1.3 copy.15
  68.8 23.8 %reduce-scatter.2.cloned.1.call-done = f32[256,256]{1,0:T(8,128)} async-done(((f32[1024,256]{1,0:T(8,128)}), f32[256,256]{1,0:T(8,128)}) %reduce-scatter.2.cloned.1.call-update) | async-done | bytes 262160 | tf_op jit(solution)/shard_map/reduce_scatter | solution.py:40
  92.7 2.0 convert_reduce_fusion
  94.9 0.9 fusion.19
  95.8 7.2 %all_gather.7 = bf16[1024,256]{1,0:T(8,128)(2,1)S(1)} all-gather(bf16[256,256]{1,0:T(8,128)(2,1)S(1)} %convolution_convert_fusion), channel_id=1, replica_groups=mesh['blk'=8,'rep'=4] {'rep'}, dimensions={0}, use_global_device_ids=true | all-gather | bytes 655360 | tf_op jit(solution)/shard_map/all_gather | solution.py:56
  103.6 1.9 multiply_bitcast_fusion
  105.5 2.3 copy.17
  107.8 78.2 %while.15 = (s32[]{:T(128)}, f32[256,256]{1,0:T(8,128)S(1)}, s32[1,16]{1,0:T(1,128)S(1)}, s32[]{:T(128)}, f32[16,128,256]{2,0,1:T(8,128)S(1)}, /*index=5*/s32[]{...) while((s32[]{:T(128)}, f32[256,256]{1,0:T(8,128)S(1)}, ...), condition=%wide.region_2.3_spmd, body=%wide.region_1.2_spmd.sunk | while | flops 12648512 | bytes 4719116 | solution.py:78
  107.9 0.8 fusion.46
  108.8 1.5 collective-permute-start
  110.3 8.3 %collective-permute-done = f32[256,256]{1,0:T(8,128)S(1)} collective-permute-done((f32[256,256]{1,0:T(8,128)S(1)}, f32[256,256]{1,0:T(8,128)S(1)}, u32[]{:S(2)}, u32[]{:S(2)}) %collective-permute-start) | collective-permute-done | bytes 262176 | tf_op jit(solution)/shard_map/while/body/eval_jaxpr/ppermute | solution.py:10
  118.6 0.8 fusion.46
  120.0 8.6 %collective-permute-done = f32[256,256]{1,0:T(8,128)S(1)} collective-permute-done((f32[256,256]{1,0:T(8,128)S(1)}, f32[256,256]{1,0:T(8,128)S(1)}, u32[]{:S(2)}, u32[]{:S(2)}) %collective-permute-start) | collective-permute-done | bytes 262176 | tf_op jit(solution)/shard_map/while/body/eval_jaxpr/ppermute | solution.py:10
  128.5 0.8 fusion.46
  129.5 7.8 %collective-permute-done = f32[256,256]{1,0:T(8,128)S(1)} collective-permute-done((f32[256,256]{1,0:T(8,128)S(1)}, f32[256,256]{1,0:T(8,128)S(1)}, u32[]{:S(2)}, u32[]{:S(2)}) %collective-permute-start) | collective-permute-done | bytes 262176 | tf_op jit(solution)/shard_map/while/body/eval_jaxpr/ppermute | solution.py:10
  137.3 0.8 fusion.46
  138.3 7.8 %collective-permute-done = f32[256,256]{1,0:T(8,128)S(1)} collective-permute-done((f32[256,256]{1,0:T(8,128)S(1)}, f32[256,256]{1,0:T(8,128)S(1)}, u32[]{:S(2)}, u32[]{:S(2)}) %collective-permute-start) | collective-permute-done | bytes 262176 | tf_op jit(solution)/shard_map/while/body/eval_jaxpr/ppermute | solution.py:10
  146.1 0.8 fusion.46
  147.1 8.3 %collective-permute-done = f32[256,256]{1,0:T(8,128)S(1)} collective-permute-done((f32[256,256]{1,0:T(8,128)S(1)}, f32[256,256]{1,0:T(8,128)S(1)}, u32[]{:S(2)}, u32[]{:S(2)}) %collective-permute-start) | collective-permute-done | bytes 262176 | tf_op jit(solution)/shard_map/while/body/eval_jaxpr/ppermute | solution.py:10
  155.4 0.8 fusion.46
  156.4 9.1 %collective-permute-done = f32[256,256]{1,0:T(8,128)S(1)} collective-permute-done((f32[256,256]{1,0:T(8,128)S(1)}, f32[256,256]{1,0:T(8,128)S(1)}, u32[]{:S(2)}, u32[]{:S(2)}) %collective-permute-start) | collective-permute-done | bytes 262176 | tf_op jit(solution)/shard_map/while/body/eval_jaxpr/ppermute | solution.py:10
  165.5 0.8 fusion.46
  166.5 9.4 %collective-permute-done = f32[256,256]{1,0:T(8,128)S(1)} collective-permute-done((f32[256,256]{1,0:T(8,128)S(1)}, f32[256,256]{1,0:T(8,128)S(1)}, u32[]{:S(2)}, u32[]{:S(2)}) %collective-permute-start) | collective-permute-done | bytes 262176 | tf_op jit(solution)/shard_map/while/body/eval_jaxpr/ppermute | solution.py:10
  175.9 0.8 fusion.46
  176.8 9.1 %collective-permute-done = f32[256,256]{1,0:T(8,128)S(1)} collective-permute-done((f32[256,256]{1,0:T(8,128)S(1)}, f32[256,256]{1,0:T(8,128)S(1)}, u32[]{:S(2)}, u32[]{:S(2)}) %collective-permute-start) | collective-permute-done | bytes 262176 | tf_op jit(solution)/shard_map/while/body/eval_jaxpr/ppermute | solution.py:10
  186.7 47.3 %psum.15 = f32[256]{0:T(256)S(1)} all-reduce(f32[256]{0:T(256)S(1)} %get-tuple-element.160), channel_id=1, replica_groups=mesh['blk'=8,'rep'=4] {'blk','rep'}, use_global_device_ids=true, to_apply=%region_5.6 | all-reduce | flops 256 | bytes 2048 | tf_op jit(solution)/shard_map/psum | solution.py:51
  234.6 1.7 broadcast_multiply_fusion
  (66 shorter events, 5.1 us)
Async XLA Ops:
  7.2 53.1 %copy-start = (bf16[1,16,128,128]{3,2,1,0:T(8,128)(2,1)S(1)}, bf16[1,16,128,128]{3,2,1,0:T(8,128)(2,1)}, u32[]{:S(2)}) copy-start(bf16[1,16,128,128]{3,2,1,0:T(8,128)(2,1)} %param.11) | copy-start | bytes 1572868
  7.2 43.2 %all-gather.2.cloned.1.call-start = ((), (), s32[]{:S(2)}) async-start(), calls=%async_computation.1 | async-start | bytes 1179648 | tf_op jit(solution)/shard_map/all_gather | solution.py:27
  7.9 84.7 %reduce-scatter.2.cloned.1.call-start = ((), (), s32[]{:S(2)}) async-start(), calls=%async_computation.2 | async-start | bytes 1310720 | tf_op jit(solution)/shard_map/reduce_scatter | solution.py:40
  62.6 2.1 copy-start.4
  67.4 25.3 %copy-start.2 = (bf16[256,256]{1,0:T(8,128)(2,1)S(1)}, bf16[256,256]{1,0:T(8,128)(2,1)}, u32[]{:S(2)}) copy-start(bf16[256,256]{1,0:T(8,128)(2,1)} %param.15) | copy-start | bytes 393220
  67.4 25.3 %copy-start.5 = (bf16[256,256]{1,0:T(8,128)(2,1)S(1)}, bf16[256,256]{1,0:T(8,128)(2,1)}, u32[]{:S(2)}) copy-start(bf16[256,256]{1,0:T(8,128)(2,1)} %param.17) | copy-start | bytes 393220
  67.4 25.2 %copy-start.6 = (f32[256]{0:T(256)S(1)}, f32[256]{0:T(256)}, u32[]{:S(2)}) copy-start(f32[256]{0:T(256)} %param.16) | copy-start | bytes 3076
  68.7 165.8 %all-reduce.2.cloned.1.call-start = ((), (), s32[]{:S(2)}) async-start(), calls=%async_computation.3 | async-start | bytes 524288 | tf_op jit(solution)/shard_map/psum | solution.py:51
  92.6 2.2 copy-start.1
  105.5 2.3 copy-start.3
  108.8 9.8 %collective-permute-start = (f32[256,256]{1,0:T(8,128)S(1)}, f32[256,256]{1,0:T(8,128)S(1)}, u32[]{:S(2)}, u32[]{:S(2)}) collective-permute-start(f32[256,256]{1,0:T(8,128)S(1)} %bitcast_add_fusion.2), channel_id=1, source_target_pairs={{28,0},{0,4},{4,8},{8,12},{12,16},{16,20},{20,24},{24,28},{29,1},{... | collective-permute-start | bytes 786440 | tf_op jit(solution)/shard_map/while/body/eval_jaxpr/ppermute | solution.py:10
  119.5 9.0 %collective-permute-start = (f32[256,256]{1,0:T(8,128)S(1)}, f32[256,256]{1,0:T(8,128)S(1)}, u32[]{:S(2)}, u32[]{:S(2)}) collective-permute-start(f32[256,256]{1,0:T(8,128)S(1)} %bitcast_add_fusion.2), channel_id=1, source_target_pairs={{28,0},{0,4},{4,8},{8,12},{12,16},{16,20},{20,24},{24,28},{29,1},{... | collective-permute-start | bytes 786440 | tf_op jit(solution)/shard_map/while/body/eval_jaxpr/ppermute | solution.py:10
  129.4 7.9 %collective-permute-start = (f32[256,256]{1,0:T(8,128)S(1)}, f32[256,256]{1,0:T(8,128)S(1)}, u32[]{:S(2)}, u32[]{:S(2)}) collective-permute-start(f32[256,256]{1,0:T(8,128)S(1)} %bitcast_add_fusion.2), channel_id=1, source_target_pairs={{28,0},{0,4},{4,8},{8,12},{12,16},{16,20},{20,24},{24,28},{29,1},{... | collective-permute-start | bytes 786440 | tf_op jit(solution)/shard_map/while/body/eval_jaxpr/ppermute | solution.py:10
  138.2 7.9 %collective-permute-start = (f32[256,256]{1,0:T(8,128)S(1)}, f32[256,256]{1,0:T(8,128)S(1)}, u32[]{:S(2)}, u32[]{:S(2)}) collective-permute-start(f32[256,256]{1,0:T(8,128)S(1)} %bitcast_add_fusion.2), channel_id=1, source_target_pairs={{28,0},{0,4},{4,8},{8,12},{12,16},{16,20},{20,24},{24,28},{29,1},{... | collective-permute-start | bytes 786440 | tf_op jit(solution)/shard_map/while/body/eval_jaxpr/ppermute | solution.py:10
  147.0 8.4 %collective-permute-start = (f32[256,256]{1,0:T(8,128)S(1)}, f32[256,256]{1,0:T(8,128)S(1)}, u32[]{:S(2)}, u32[]{:S(2)}) collective-permute-start(f32[256,256]{1,0:T(8,128)S(1)} %bitcast_add_fusion.2), channel_id=1, source_target_pairs={{28,0},{0,4},{4,8},{8,12},{12,16},{16,20},{20,24},{24,28},{29,1},{... | collective-permute-start | bytes 786440 | tf_op jit(solution)/shard_map/while/body/eval_jaxpr/ppermute | solution.py:10
  156.3 9.2 %collective-permute-start = (f32[256,256]{1,0:T(8,128)S(1)}, f32[256,256]{1,0:T(8,128)S(1)}, u32[]{:S(2)}, u32[]{:S(2)}) collective-permute-start(f32[256,256]{1,0:T(8,128)S(1)} %bitcast_add_fusion.2), channel_id=1, source_target_pairs={{28,0},{0,4},{4,8},{8,12},{12,16},{16,20},{20,24},{24,28},{29,1},{... | collective-permute-start | bytes 786440 | tf_op jit(solution)/shard_map/while/body/eval_jaxpr/ppermute | solution.py:10
  166.4 9.5 %collective-permute-start = (f32[256,256]{1,0:T(8,128)S(1)}, f32[256,256]{1,0:T(8,128)S(1)}, u32[]{:S(2)}, u32[]{:S(2)}) collective-permute-start(f32[256,256]{1,0:T(8,128)S(1)} %bitcast_add_fusion.2), channel_id=1, source_target_pairs={{28,0},{0,4},{4,8},{8,12},{12,16},{16,20},{20,24},{24,28},{29,1},{... | collective-permute-start | bytes 786440 | tf_op jit(solution)/shard_map/while/body/eval_jaxpr/ppermute | solution.py:10
  176.8 9.2 %collective-permute-start = (f32[256,256]{1,0:T(8,128)S(1)}, f32[256,256]{1,0:T(8,128)S(1)}, u32[]{:S(2)}, u32[]{:S(2)}) collective-permute-start(f32[256,256]{1,0:T(8,128)S(1)} %bitcast_add_fusion.2), channel_id=1, source_target_pairs={{28,0},{0,4},{4,8},{8,12},{12,16},{16,20},{20,24},{24,28},{29,1},{... | collective-permute-start | bytes 786440 | tf_op jit(solution)/shard_map/while/body/eval_jaxpr/ppermute | solution.py:10
Sparse Core Ops, SparseCore 0:
  10.1 40.2 all-gather.1
  68.9 23.7 reduce-scatter.1
  98.7 131.8 all-reduce.1
where the time goes:
time: 243 us
  waiting for transfers between devices  134 us (55%)
  blocking collectives  54.5 us (22%)
  matrix products  16.7 us (7%)
  local copies, waits for them, and re-layouts  16.3 us (7%)
  between operations  14.6 us (6%)
  other arithmetic  4.1 us (2%)
  starting transfers between devices  2.45 us (1%)
    ppermute x8, waiting for transfers between devices, shifted(): return lax.ppermute(block, axis, route)  68.5 us
    psum x1, blocking collectives, per_device(): lax.psum((local_weight, local_bias), ('blk', 'rep'))  47.3 us
    all_gather x1, waiting for transfers between devices, per_device(): piece = lax.all_gather(features, 'blk', axis=0, tiled=True)  40.9 us
    reduce_scatter x1, waiting for transfers between devices, per_device(): lax.psum_scatter(summed.reshape(rep_count * own_rows, feat_width), 'rep',...  23.8 us
    gather x1, local copies, waits for them, and re-layouts, per_device(): jnp.take(piece, clipped.reshape(-1), axis=0)  9.83 us
    all_gather x1, blocking collectives, per_device(): lax.all_gather(agg_grad, 'rep', axis=0, tiled=True)  7.17 us
    dot_general x8, matrix products, column_terms(): jnp.einsum('sp,sjf->pjf', col_onehot, contribution, precision=highest)  6.58 us
  transfers between devices with their start and end apart: 11, of which 10 were waited for; matrix products, arithmetic and copies ran while one was open for 6% of the time, Pallas kernels for 0%

commit v1 on v0

--- a/solution.py
+++ b/solution.py
@@ -2,6 +2,11 @@
 import jax.numpy as jnp
 from jax import lax
 from jax.sharding import PartitionSpec as P
+
+
+def supply_all_leaves(state):
+    o_now = lax.psum(lax.psum(state, axis_name="rep"), "blk")
+    return o_now
 
 
 def shifted(block, axis, distance):
@@ -48,7 +53,7 @@
     ).astype(jnp.bfloat16)
     local_weight = jnp.dot(aggregate.T, act_grad, preferred_element_type=jnp.float32)
     local_bias = jnp.sum(act_grad.astype(jnp.float32), axis=0)
-    weight_grad, bias_grad = lax.psum((local_weight, local_bias), ("blk", "rep"))
+    weight_grad, bias_grad = supply_all_leaves((local_weight, local_bias))
     scale_factor = 1.0 / (blk_count * rep_count)
     weight_grad = weight_grad * scale_factor
     bias_grad = bias_grad * scale_factor

time: 243 us -> 253 us (1.041)
  the two profiles are of different devices: /device:TPU:10 before, /device:TPU:0 now
where the time goes in v1:
time: 253 us
  waiting for transfers between devices  169 us (67%)
  blocking collectives  29.5 us (12%)
  matrix products  16.7 us (7%)
  local copies, waits for them, and re-layouts  16.2 us (6%)
  between operations  14.6 us (6%)
  other arithmetic  4.11 us (2%)
    ppermute x8, waiting for transfers between devices, shifted(): return lax.ppermute(block, axis, route)  80.3 us
    all_gather x1, waiting for transfers between devices, per_device(): piece = lax.all_gather(features, 'blk', axis=0, tiled=True)  43.7 us
    reduce_scatter x1, waiting for transfers between devices, per_device(): lax.psum_scatter(summed.reshape(rep_count * own_rows, feat_width), 'rep',...  23.6 us
    psum x2, blocking collectives, supply_all_leaves(): o_now = lax.psum(lax.psum(state, axis_name='rep'), 'blk')  22.8 us
    psum x2, waiting for transfers between devices, supply_all_leaves(): o_now = lax.psum(lax.psum(state, axis_name='rep'), 'blk')  21 us
    gather x1, local copies, waits for them, and re-layouts, per_device(): jnp.take(piece, clipped.reshape(-1), axis=0)  9.81 us
    all_gather x1, blocking collectives, per_device(): lax.all_gather(agg_grad, 'rep', axis=0, tiled=True)  6.61 us
    dot_general x8, matrix products, column_terms(): jnp.einsum('sp,sjf->pjf', col_onehot, contribution, precision=highest)  6.58 us
  transfers between devices with their start and end apart: 12, of which 11 were waited for; matrix products, arithmetic and copies ran while one was open for 6% of the time, Pallas kernels for 0%

profile of v1, /device:TPU:0, one launch (start us, length us, event | category | flops | bytes accessed | tf_op | source)
XLA Modules:
  0.0 252.6 jit_solution(17024513736372025570)
XLA Ops:
  9.5 43.7 %all-gather.2.cloned.1.call-done = bf16[2048,256]{1,0:T(8,128)(2,1)} async-done(((bf16[256,256]{1,0:T(8,128)(2,1)}), bf16[2048,256]{1,0:T(8,128)(2,1)}) %all-gather.2.cloned.1.call-update) | async-done | bytes 1048592 | tf_op jit(solution)/shard_map/all_gather | solution.py:32
  53.1 9.8 %gather_fusion = bf16[2048,256]{1,0:T(8,128)(2,1)} fusion(bf16[2048,256]{1,0:T(8,128)(2,1)} %all-gather.2.cloned.1.call-done, s32[2048]{0:T(1024)S(1)} %broadcast_clamp_fusion), kind=kCustom, calls=%fused_computation | custom fusion | bytes 2105344 | tf_op jit(solution)/shard_map/jit(_take)/gather | solution.py:36
  63.0 2.3 fusion.8
  65.3 2.1 copy.18
  67.4 2.7 %fusion.5 = f32[8,128,256]{2,0,1:T(8,128)S(1)} fusion(f32[16,256,128]{1,0,2:T(8,128)} %copy.18, f32[16]{0:T(128)S(1)} %compare_convert_fusion, s32[16]{0:T(128)S(1)} %bitcast.53), kind=kOutput, calls=%fused_computation.9 | convolution fusion | flops 50331904 | bytes 3145856 | tf_op jit(solution)/shard_map/st,sif->tif/dot_general | solution.py:44
  70.1 1.3 copy.15
  71.5 23.6 %reduce-scatter.2.cloned.1.call-done = f32[256,256]{1,0:T(8,128)} async-done(((f32[1024,256]{1,0:T(8,128)}), f32[256,256]{1,0:T(8,128)}) %reduce-scatter.2.cloned.1.call-update) | async-done | bytes 262160 | tf_op jit(solution)/shard_map/reduce_scatter | solution.py:45
  95.1 2.0 convert_reduce_fusion
  97.3 0.9 fusion.19
  98.3 6.6 %all_gather.7 = bf16[1024,256]{1,0:T(8,128)(2,1)S(1)} all-gather(bf16[256,256]{1,0:T(8,128)(2,1)S(1)} %convolution_convert_fusion), channel_id=1, replica_groups=mesh['blk'=8,'rep'=4] {'rep'}, dimensions={0}, use_global_device_ids=true | all-gather | bytes 655360 | tf_op jit(solution)/shard_map/all_gather | solution.py:61
  105.6 1.9 multiply_bitcast_fusion
  107.5 2.3 copy.17
  109.7 21.0 %all-reduce.3.cloned.1.call-done = f32[256,256]{1,0:T(8,128)} async-done(((f32[256,256]{1,0:T(8,128)}), f32[256,256]{1,0:T(8,128)}) %all-reduce.3.cloned.1.call-update) | async-done | bytes 262160 | tf_op jit(solution)/shard_map/psum | solution.py:8
  130.8 89.6 %while.15 = (s32[]{:T(128)}, f32[256,256]{1,0:T(8,128)S(1)}, s32[1,16]{1,0:T(1,128)S(1)}, s32[]{:T(128)}, f32[16,128,256]{2,0,1:T(8,128)S(1)}, /*index=5*/s32[]{...) while((s32[]{:T(128)}, f32[256,256]{1,0:T(8,128)S(1)}, ...), condition=%wide.region_2.3_spmd, body=%wide.region_1.2_spmd.sunk | while | flops 12648512 | bytes 4719116 | solution.py:83
  131.7 1.5 collective-permute-start
  133.3 7.9 %collective-permute-done = f32[256,256]{1,0:T(8,128)S(1)} collective-permute-done((f32[256,256]{1,0:T(8,128)S(1)}, f32[256,256]{1,0:T(8,128)S(1)}, u32[]{:S(2)}, u32[]{:S(2)}) %collective-permute-start) | collective-permute-done | bytes 262176 | tf_op jit(solution)/shard_map/while/body/eval_jaxpr/ppermute | solution.py:15
  141.2 0.8 fusion.46
  142.2 10.6 %collective-permute-done = f32[256,256]{1,0:T(8,128)S(1)} collective-permute-done((f32[256,256]{1,0:T(8,128)S(1)}, f32[256,256]{1,0:T(8,128)S(1)}, u32[]{:S(2)}, u32[]{:S(2)}) %collective-permute-start) | collective-permute-done | bytes 262176 | tf_op jit(solution)/shard_map/while/body/eval_jaxpr/ppermute | solution.py:15
  152.7 0.8 fusion.46
  153.7 9.3 %collective-permute-done = f32[256,256]{1,0:T(8,128)S(1)} collective-permute-done((f32[256,256]{1,0:T(8,128)S(1)}, f32[256,256]{1,0:T(8,128)S(1)}, u32[]{:S(2)}, u32[]{:S(2)}) %collective-permute-start) | collective-permute-done | bytes 262176 | tf_op jit(solution)/shard_map/while/body/eval_jaxpr/ppermute | solution.py:15
  163.0 0.8 fusion.46
  164.0 9.1 %collective-permute-done = f32[256,256]{1,0:T(8,128)S(1)} collective-permute-done((f32[256,256]{1,0:T(8,128)S(1)}, f32[256,256]{1,0:T(8,128)S(1)}, u32[]{:S(2)}, u32[]{:S(2)}) %collective-permute-start) | collective-permute-done | bytes 262176 | tf_op jit(solution)/shard_map/while/body/eval_jaxpr/ppermute | solution.py:15
  173.1 0.8 fusion.46
  174.1 9.9 %collective-permute-done = f32[256,256]{1,0:T(8,128)S(1)} collective-permute-done((f32[256,256]{1,0:T(8,128)S(1)}, f32[256,256]{1,0:T(8,128)S(1)}, u32[]{:S(2)}, u32[]{:S(2)}) %collective-permute-start) | collective-permute-done | bytes 262176 | tf_op jit(solution)/shard_map/while/body/eval_jaxpr/ppermute | solution.py:15
  184.0 0.8 fusion.46
  185.0 10.4 %collective-permute-done = f32[256,256]{1,0:T(8,128)S(1)} collective-permute-done((f32[256,256]{1,0:T(8,128)S(1)}, f32[256,256]{1,0:T(8,128)S(1)}, u32[]{:S(2)}, u32[]{:S(2)}) %collective-permute-start) | collective-permute-done | bytes 262176 | tf_op jit(solution)/shard_map/while/body/eval_jaxpr/ppermute | solution.py:15
  196.4 13.9 %collective-permute-done = f32[256,256]{1,0:T(8,128)S(1)} collective-permute-done((f32[256,256]{1,0:T(8,128)S(1)}, f32[256,256]{1,0:T(8,128)S(1)}, u32[]{:S(2)}, u32[]{:S(2)}) %collective-permute-start) | collective-permute-done | bytes 262176 | tf_op jit(solution)/shard_map/while/body/eval_jaxpr/ppermute | solution.py:15
  210.3 0.8 fusion.46
  211.3 9.1 %collective-permute-done = f32[256,256]{1,0:T(8,128)S(1)} collective-permute-done((f32[256,256]{1,0:T(8,128)S(1)}, f32[256,256]{1,0:T(8,128)S(1)}, u32[]{:S(2)}, u32[]{:S(2)}) %collective-permute-start) | collective-permute-done | bytes 262176 | tf_op jit(solution)/shard_map/while/body/eval_jaxpr/ppermute | solution.py:15
  221.0 5.7 %psum.30 = f32[256]{0:T(256)S(1)} all-reduce(f32[256]{0:T(256)S(1)} %get-tuple-element.160), channel_id=1, replica_groups=mesh['blk'=8,'rep'=4] {'rep'}, use_global_device_ids=true, to_apply=%region_6.7 | all-reduce | flops 256 | bytes 2048 | tf_op jit(solution)/shard_map/psum | solution.py:8
  226.8 17.1 %psum.31 = f32[256]{0:T(256)S(1)} all-reduce(f32[256]{0:T(256)S(1)} %psum.30), channel_id=1, replica_groups=mesh['blk'=8,'rep'=4] {'blk'}, use_global_device_ids=true, to_apply=%region_7.8 | all-reduce | flops 256 | bytes 2048 | tf_op jit(solution)/shard_map/psum | solution.py:8
  244.4 1.7 broadcast_multiply_fusion
  (70 shorter events, 6.4 us)
Async XLA Ops:
  7.2 55.8 %copy-start = (bf16[1,16,128,128]{3,2,1,0:T(8,128)(2,1)S(1)}, bf16[1,16,128,128]{3,2,1,0:T(8,128)(2,1)}, u32[]{:S(2)}) copy-start(bf16[1,16,128,128]{3,2,1,0:T(8,128)(2,1)} %param.11) | copy-start | bytes 1572868
  7.2 46.0 %all-gather.2.cloned.1.call-start = ((), (), s32[]{:S(2)}) async-start(), calls=%async_computation.1 | async-start | bytes 1179648 | tf_op jit(solution)/shard_map/all_gather | solution.py:32
  7.9 87.2 %reduce-scatter.2.cloned.1.call-start = ((), (), s32[]{:S(2)}) async-start(), calls=%async_computation.2 | async-start | bytes 1310720 | tf_op jit(solution)/shard_map/reduce_scatter | solution.py:45
  65.3 2.1 copy-start.4
  70.1 25.0 %copy-start.2 = (bf16[256,256]{1,0:T(8,128)(2,1)S(1)}, bf16[256,256]{1,0:T(8,128)(2,1)}, u32[]{:S(2)}) copy-start(bf16[256,256]{1,0:T(8,128)(2,1)} %param.15) | copy-start | bytes 393220
  70.1 25.0 %copy-start.5 = (bf16[256,256]{1,0:T(8,128)(2,1)S(1)}, bf16[256,256]{1,0:T(8,128)(2,1)}, u32[]{:S(2)}) copy-start(bf16[256,256]{1,0:T(8,128)(2,1)} %param.17) | copy-start | bytes 393220
  70.1 25.0 %copy-start.6 = (f32[256]{0:T(256)S(1)}, f32[256]{0:T(256)}, u32[]{:S(2)}) copy-start(f32[256]{0:T(256)} %param.16) | copy-start | bytes 3076
  71.4 59.3 %all-reduce.3.cloned.1.call-start = ((), (), s32[]{:S(2)}) async-start(), calls=%async_computation.3 | async-start | bytes 524288 | tf_op jit(solution)/shard_map/psum | solution.py:8
  95.1 2.2 copy-start.1
  98.3 146.2 %all-reduce.5.cloned.1.call-start = ((), (), s32[]{:S(2)}) async-start(), calls=%async_computation.4 | async-start | bytes 524288 | tf_op jit(solution)/shard_map/psum | solution.py:8
  107.5 23.3 %copy-start.3 = (s32[1,16]{1,0:T(1,128)S(1)}, s32[1,16]{1,0:T(1,128)}, u32[]{:S(2)}) copy-start(s32[1,16]{1,0:T(1,128)} %param.13) | copy-start | bytes 196
  131.7 9.4 %collective-permute-start = (f32[256,256]{1,0:T(8,128)S(1)}, f32[256,256]{1,0:T(8,128)S(1)}, u32[]{:S(2)}, u32[]{:S(2)}) collective-permute-start(f32[256,256]{1,0:T(8,128)S(1)} %bitcast_add_fusion.2), channel_id=1, source_target_pairs={{28,0},{0,4},{4,8},{8,12},{12,16},{16,20},{20,24},{24,28},{29,1},{... | collective-permute-start | bytes 786440 | tf_op jit(solution)/shard_map/while/body/eval_jaxpr/ppermute | solution.py:15
  142.1 10.6 %collective-permute-start = (f32[256,256]{1,0:T(8,128)S(1)}, f32[256,256]{1,0:T(8,128)S(1)}, u32[]{:S(2)}, u32[]{:S(2)}) collective-permute-start(f32[256,256]{1,0:T(8,128)S(1)} %bitcast_add_fusion.2), channel_id=1, source_target_pairs={{28,0},{0,4},{4,8},{8,12},{12,16},{16,20},{20,24},{24,28},{29,1},{... | collective-permute-start | bytes 786440 | tf_op jit(solution)/shard_map/while/body/eval_jaxpr/ppermute | solution.py:15
  153.6 9.4 %collective-permute-start = (f32[256,256]{1,0:T(8,128)S(1)}, f32[256,256]{1,0:T(8,128)S(1)}, u32[]{:S(2)}, u32[]{:S(2)}) collective-permute-start(f32[256,256]{1,0:T(8,128)S(1)} %bitcast_add_fusion.2), channel_id=1, source_target_pairs={{28,0},{0,4},{4,8},{8,12},{12,16},{16,20},{20,24},{24,28},{29,1},{... | collective-permute-start | bytes 786440 | tf_op jit(solution)/shard_map/while/body/eval_jaxpr/ppermute | solution.py:15
  163.9 9.2 %collective-permute-start = (f32[256,256]{1,0:T(8,128)S(1)}, f32[256,256]{1,0:T(8,128)S(1)}, u32[]{:S(2)}, u32[]{:S(2)}) collective-permute-start(f32[256,256]{1,0:T(8,128)S(1)} %bitcast_add_fusion.2), channel_id=1, source_target_pairs={{28,0},{0,4},{4,8},{8,12},{12,16},{16,20},{20,24},{24,28},{29,1},{... | collective-permute-start | bytes 786440 | tf_op jit(solution)/shard_map/while/body/eval_jaxpr/ppermute | solution.py:15
  174.0 10.0 %collective-permute-start = (f32[256,256]{1,0:T(8,128)S(1)}, f32[256,256]{1,0:T(8,128)S(1)}, u32[]{:S(2)}, u32[]{:S(2)}) collective-permute-start(f32[256,256]{1,0:T(8,128)S(1)} %bitcast_add_fusion.2), channel_id=1, source_target_pairs={{28,0},{0,4},{4,8},{8,12},{12,16},{16,20},{20,24},{24,28},{29,1},{... | collective-permute-start | bytes 786440 | tf_op jit(solution)/shard_map/while/body/eval_jaxpr/ppermute | solution.py:15
  184.9 10.5 %collective-permute-start = (f32[256,256]{1,0:T(8,128)S(1)}, f32[256,256]{1,0:T(8,128)S(1)}, u32[]{:S(2)}, u32[]{:S(2)}) collective-permute-start(f32[256,256]{1,0:T(8,128)S(1)} %bitcast_add_fusion.2), channel_id=1, source_target_pairs={{28,0},{0,4},{4,8},{8,12},{12,16},{16,20},{20,24},{24,28},{29,1},{... | collective-permute-start | bytes 786440 | tf_op jit(solution)/shard_map/while/body/eval_jaxpr/ppermute | solution.py:15
  196.3 14.0 %collective-permute-start = (f32[256,256]{1,0:T(8,128)S(1)}, f32[256,256]{1,0:T(8,128)S(1)}, u32[]{:S(2)}, u32[]{:S(2)}) collective-permute-start(f32[256,256]{1,0:T(8,128)S(1)} %bitcast_add_fusion.2), channel_id=1, source_target_pairs={{28,0},{0,4},{4,8},{8,12},{12,16},{16,20},{20,24},{24,28},{29,1},{... | collective-permute-start | bytes 786440 | tf_op jit(solution)/shard_map/while/body/eval_jaxpr/ppermute | solution.py:15
  211.2 9.1 %collective-permute-start = (f32[256,256]{1,0:T(8,128)S(1)}, f32[256,256]{1,0:T(8,128)S(1)}, u32[]{:S(2)}, u32[]{:S(2)}) collective-permute-start(f32[256,256]{1,0:T(8,128)S(1)} %bitcast_add_fusion.2), channel_id=1, source_target_pairs={{28,0},{0,4},{4,8},{8,12},{12,16},{16,20},{20,24},{24,28},{29,1},{... | collective-permute-start | bytes 786440 | tf_op jit(solution)/shard_map/while/body/eval_jaxpr/ppermute | solution.py:15
Sparse Core Ops, SparseCore 0:
  10.1 42.9 all-gather.1
  71.6 23.4 reduce-scatter.1
  98.4 32.2 all-reduce.2
  133.9 75.5 all-reduce.4
